TPU v7x, 32 devices: a whole 2x2x4 slice. The times are simulated.
32 devices in a mesh: grp: 2 (over y), ti: 4 (over x, core), tj: 4 (over z).
Axes of the slice: x: 2, y: 2, z: 4, core: 2. Of those that a mesh axis runs over, the one named last changes fastest.
Arguments:
- corpus: bfloat16 [2, 24576, 1024], P('grp', ('ti', 'tj')), may hold values from -64 to 64
- slot_of_row: int32 [2, 24576], P('grp', ('ti', 'tj')), may hold values from -1 to 24575, as said below
Outputs:
- max_similarity: float32 [2, 12288], P('grp', ('ti', 'tj'))
Inputs may be any that keep to these rules, and one draw needn't show every extreme that they name: `slot_of_row`: every value from 0 to 24575 appears exactly once; a row with value v lies on a device whose ti index is (v % 12288) // 3072; from one device at most 192 rows have values in one aligned group of 768 consecutive values, and some device sends exactly 192 to some group.
All inputs are finite; a program needn't handle non-finite values.
Results may differ from a plain program's by a relative error of at most 0.0009.
Values may be sent and summed in bfloat16 or wider, within the bound.
A program may use at most 64 MiB of HBM per device.

v0:
```python
import jax
import jax.numpy as jnp
from jax import lax
from jax.sharding import PartitionSpec as P

BLK = 3072


epsilon = 1e-06


def per_device(corpus, slot_of_row):
    rows_in = corpus[0]
    values = slot_of_row[0]
    src_count = values.shape[0]
    features = rows_in.shape[1]
    lane_count = lax.axis_size("tj")
    sub_rows = src_count // 2
    cluster = BLK * lax.axis_size("ti")
    capacity = BLK // (lane_count * lane_count)
    owners = 2 * lane_count
    member = values >= 0
    inside = values % cluster
    grid_of = values // cluster
    sub_index = inside % BLK // sub_rows
    owner_of = jnp.where(member, grid_of * lane_count + sub_index, owners)
    onehot = (owner_of[:, None] == jnp.arange(owners, dtype=jnp.int32)[None, :]).astype(jnp.int32)
    rank_in = jnp.sum((jnp.cumsum(onehot, axis=0) - onehot) * onehot, axis=1)
    slot_pos = jnp.where(member, owner_of * capacity + rank_in, owners * capacity)
    send_rows = (
        jnp.zeros((owners * capacity, features), rows_in.dtype)
        .at[slot_pos]
        .set(rows_in, mode="drop")
    )
    send_ids = (
        jnp.full((owners * capacity,), sub_rows, jnp.int32)
        .at[slot_pos]
        .set(inside % sub_rows, mode="drop")
    )
    got_rows, got_ids = (
        lax.all_to_all(
            send_rows.reshape(owners, capacity, features),
            ("grp", "tj"),
            split_axis=0,
            concat_axis=0,
            tiled=True,
        ),
        lax.all_to_all(
            send_ids.reshape(owners, capacity),
            ("grp", "tj"),
            split_axis=0,
            concat_axis=0,
            tiled=True,
        ),
    )
    arrived = (
        jnp.zeros((sub_rows, features), rows_in.dtype)
        .at[got_ids.reshape(-1)]
        .set(got_rows.reshape(-1, features), mode="drop")
    )
    widened = arrived.astype(jnp.float32)
    row_squares = jnp.sum(widened * widened, axis=1, keepdims=True)
    inverse_norm = lax.rsqrt(row_squares + epsilon)
    unit_rows = (widened * inverse_norm).astype(jnp.bfloat16)
    tile_row = lax.axis_index("ti")
    tile_col = lax.axis_index("tj")
    block_rows = lax.all_gather(unit_rows, "tj", axis=0, tiled=True)
    row_slot = tile_row * BLK + jnp.arange(BLK, dtype=jnp.int32)
    portion = lax.all_gather(unit_rows, "ti", axis=0, tiled=True)
    length = portion.shape[0]
    position = jnp.arange(length, dtype=jnp.int32)
    col_slot = position // sub_rows * BLK + tile_col * sub_rows + position % sub_rows
    scores = lax.dot_general(
        block_rows, portion, (((1,), (1,)), ((), ())), preferred_element_type=jnp.float32
    )
    scores = jnp.where(row_slot[:, None] == col_slot[None, :], -2.0, scores)
    tile_best = jnp.maximum(jnp.full((BLK,), -2.0, jnp.float32), jnp.max(scores, axis=1))
    combined = lax.pmax(tile_best, "tj")
    result = lax.dynamic_slice_in_dim(combined, tile_col * sub_rows, sub_rows, 0)
    return result[None, :]


def solution(mesh):
    in_specs = (P("grp", ("ti", "tj"), None), P("grp", ("ti", "tj")))
    out_specs = P("grp", ("ti", "tj"))
    return jax.shard_map(
        per_device, mesh=mesh, in_specs=in_specs, out_specs=out_specs, check_vma=False
    )
```

profile of v0, /device:TPU:0, one launch (start us, length us, event | category | flops | bytes accessed | tf_op | source)
XLA Modules:
  0.0 336.0 jit_solution(1104900848834688039)
XLA Ops:
  6.5 0.9 fusion.39
  7.4 0.8 compare_reduce_fusion.1
  8.3 2.3 reduce-window.6
  10.6 0.3 slice_reduce_fusion
  10.9 0.2 reduce-window.9
  11.1 0.1 add_bitcast_fusion
  11.2 0.8 fusion.32
  12.0 6.2 %scatter_custom_fusion = s32[1536]{0:T(1024)S(1)} fusion(s32[1536]{0:T(1024)S(1)} %fusion.32, s32[1536]{0:T(1024)S(1)} %get-tuple-element.9, s32[]{:T(128)} %constant.74.clone.1), kind=kCustom, calls=%fused_computation.82 | custom fusion | bytes 6148 | tf_op jit(solution)/shard_map/scatter | solution.py:38
  18.2 0.7 all_to_all.9
  18.9 7.3 %all-to-all-start = ((s32[8,1,192]{2,1,0:T(1,128)}), s32[8,1,192]{2,1,0:T(1,128)S(1)}, u32[]{:S(2)}, u32[]{:S(2)}) async-start(s32[8,1,192]{2,1,0:T(1,128)} %all_to_all.9), calls=%async_computation | async-start | bytes 16384 | tf_op jit(solution)/shard_map/all_to_all | solution.py:48
  26.2 9.7 %scatter_custom_fusion.1 = bf16[1536,1024]{1,0:T(8,128)(2,1)} fusion(s32[1536]{0:T(1024)S(1)} %fusion.32, bf16[1,1536,1024]{2,1,0:T(8,128)(2,1)S(1)} %copy-done, bf16[]{:T(256)} %constant.78.clone.1), kind=kCustom, calls=%fused_computation.8 | custom fusion | bytes 6291458 | tf_op jit(solution)/shard_map/scatter | solution.py:33
  35.9 6.0 %all-to-all-start.1 = ((bf16[8,192,1024]{2,1,0:T(8,128)(2,1)}), bf16[8,192,1024]{2,1,0:T(8,128)(2,1)}, u32[]{:S(2)}, u32[]{:S(2)}) async-start(bf16[8,192,1024]{2,1,0:T(8,128)(2,1)} %bitcast.80), calls=%async_computation.1 | async-start | bytes 6291456 | tf_op jit(solution)/shard_map/all_to_all | solution.py:41
  42.0 0.1 reshape.266
  42.1 70.9 %all-to-all-done.1 = bf16[8,192,1024]{2,1,0:T(8,128)(2,1)} async-done(((bf16[8,192,1024]{2,1,0:T(8,128)(2,1)}), bf16[8,192,1024]{2,1,0:T(8,128)(2,1)}, u32[]{:S(2)}, u32[]{:S(2)}) %all-to-all-start.1) | async-done | bytes 3145760 | tf_op jit(solution)/shard_map/all_to_all | solution.py:41
  113.0 9.5 %scatter_custom_fusion.2 = bf16[768,1024]{1,0:T(8,128)(2,1)} fusion(s32[1536]{0:T(1024)S(1)} %fusion.33, bf16[1536,1024]{1,0:T(8,128)(2,1)} %bitcast.7, bf16[]{:T(256)} %constant.78.clone.1), kind=kCustom, calls=%fused_computation.11 | custom fusion | bytes 1573376 | tf_op jit(solution)/shard_map/scatter | solution.py:59
  122.5 1.8 fusion
  124.2 2.9 fusion.1
  127.2 0.2 all-gather.5.cloned.1.call-start
  127.4 0.5 all-gather.5.cloned.1.call-update
  128.0 112.0 %all-gather.3.cloned.1.call-done = bf16[3072,1024]{1,0:T(8,128)(2,1)} async-done(((bf16[768,1024]{1,0:T(8,128)(2,1)}), bf16[3072,1024]{1,0:T(8,128)(2,1)}) %all-gather.3.cloned.1.call-update) | async-done | bytes 6291472 | tf_op jit(solution)/shard_map/all_gather | solution.py:67
  240.0 46.1 %all-gather.5.cloned.1.call-done = bf16[3072,1024]{1,0:T(8,128)(2,1)} async-done(((bf16[768,1024]{1,0:T(8,128)(2,1)}), bf16[3072,1024]{1,0:T(8,128)(2,1)}) %all-gather.5.cloned.1.call-update) | async-done | bytes 6291472 | tf_op jit(solution)/shard_map/all_gather | solution.py:69
  286.2 23.7 %select_reduce_fusion = f32[3072]{0:T(1024)S(1)} fusion(bf16[3072,1024]{1,0:T(8,128)(2,1)} %all-gather.3.cloned.1.call-done, bf16[3072,1024]{1,0:T(8,128)(2,1)} %all-gather.5.cloned.1.call-done, s32[3072]{0:T(1024)S(1)} %iota_add_fusion, s32[3072]{0:T(1024)S(1)} %fusion.20), kind=kOutput, calls=%fused_computation.3 | convolution fusion | flops 19355660288 | bytes 12619776 | tf_op jit(solution)/shard_map/dot_general | solution.py:73
  309.8 18.7 %pmax.7 = f32[3072]{0:T(1024)S(1)} all-reduce(f32[3072]{0:T(1024)S(1)} %broadcast_maximum_fusion), channel_id=1, replica_groups=mesh['grp'=2,'ti'=4,'tj'=4] {'tj'}, use_global_device_ids=true, to_apply=%region_8.9 | all-reduce | flops 3072 | bytes 24576 | tf_op jit(solution)/shard_map/pmax | solution.py:78
  328.6 0.6 broadcast_in_dim.43
  (16 shorter events, 0.3 us)
Async XLA Ops:
  6.5 19.7 %copy-start = (bf16[1,1536,1024]{2,1,0:T(8,128)(2,1)S(1)}, bf16[1,1536,1024]{2,1,0:T(8,128)(2,1)}, u32[]{:S(2)}) copy-start(bf16[1,1536,1024]{2,1,0:T(8,128)(2,1)} %param.2) | copy-start | bytes 9437188
  18.9 17.0 %all-to-all-start = ((s32[8,1,192]{2,1,0:T(1,128)}), s32[8,1,192]{2,1,0:T(1,128)S(1)}, u32[]{:S(2)}, u32[]{:S(2)}) async-start(s32[8,1,192]{2,1,0:T(1,128)} %all_to_all.9), calls=%async_computation | async-start | bytes 16384 | tf_op jit(solution)/shard_map/all_to_all | solution.py:48
  35.9 77.1 %all-to-all-start.1 = ((bf16[8,192,1024]{2,1,0:T(8,128)(2,1)}), bf16[8,192,1024]{2,1,0:T(8,128)(2,1)}, u32[]{:S(2)}, u32[]{:S(2)}) async-start(bf16[8,192,1024]{2,1,0:T(8,128)(2,1)} %bitcast.80), calls=%async_computation.1 | async-start | bytes 6291456 | tf_op jit(solution)/shard_map/all_to_all | solution.py:41
  41.9 198.1 %all-gather.3.cloned.1.call-start = ((), (), s32[]{:S(2)}) async-start(), calls=%async_computation.2 | async-start | bytes 7864320 | tf_op jit(solution)/shard_map/all_gather | solution.py:67
  127.2 159.0 %all-gather.5.cloned.1.call-start = ((), (), s32[]{:S(2)}) async-start(), calls=%async_computation.3 | async-start | bytes 7864320 | tf_op jit(solution)/shard_map/all_gather | solution.py:69
Sparse Core Ops, SparseCore 0:
  127.3 112.6 all-gather.2
  241.6 44.5 all-gather.4
where the time goes:
time: 336 us
  waiting for transfers between devices  230 us (68%)
  local copies, waits for them, and re-layouts  27 us (8%)
  matrix products  23.7 us (7%)
  blocking collectives  18.7 us (6%)
  starting transfers between devices  13.6 us (4%)
  between operations  13.5 us (4%)
  other arithmetic  9.96 us (3%)
    all_gather x1, waiting for transfers between devices, per_device(): block_rows = lax.all_gather(unit_rows, 'tj', axis=0, tiled=True)  112 us
    all_to_all x1, waiting for transfers between devices, per_device(): lax.all_to_all(send_rows.reshape(owners, capacity, features), ('grp', 'tj...  70.9 us
    all_gather x1, waiting for transfers between devices, per_device(): portion = lax.all_gather(unit_rows, 'ti', axis=0, tiled=True)  46.1 us
    dot_general x1, matrix products, per_device(): lax.dot_general(block_rows, portion, (((1,), (1,)), ((), ())), preferred_...  23.7 us
    pmax x1, blocking collectives, per_device(): combined = lax.pmax(tile_best, 'tj')  18.7 us
    scatter x1, local copies, waits for them, and re-layouts, per_device(): send_rows = jnp.zeros((owners * capacity, features), rows_in.dtype).at[sl...  9.66 us
    scatter x1, local copies, waits for them, and re-layouts, per_device(): arrived = jnp.zeros((sub_rows, features), rows_in.dtype).at[got_ids.resha...  9.47 us
    all_to_all x1, starting transfers between devices, per_device(): lax.all_to_all(send_ids.reshape(owners, capacity), ('grp', 'tj'), split_a...  7.31 us
  transfers between devices with their start and end apart: 4, of which 3 were waited for; matrix products, arithmetic and copies ran while one was open for 3% of the time, Pallas kernels for 0%

commit v1 on v0

v1 whole, which is shorter than its diff:
```python
import functools

import jax
import jax.numpy as jnp
from jax import lax
from jax.experimental import pallas as pl
from jax.experimental.pallas import tpu as pltpu
from jax.sharding import PartitionSpec as P

MESH = pl.DeviceIdType.MESH
NT = (((1,), (1,)), ((), ()))
NN = (((1,), (0,)), ((), ()))
CORES = 2
EPSILON = 1e-06


def dot(a, b, dims):
    return lax.dot_general(a, b, dims, preferred_element_type=jnp.float32)


def kernel(geo, slots_ref, corpus_ref, out_ref, spot, ids_src, send, send_ids, got, got_ids,
           summed, rows, cols, best, parts, s_send, s_recv, i_send, i_recv,
           r_send, r_recv, c_send, c_recv, p_send, p_recv):
    ti_count, tj_count, count, features, sub, cap, chunks = geo
    owners = 2 * tj_count
    xs = ti_count // CORES
    zs = tj_count // 2
    blk = sub * tj_count
    cluster = blk * ti_count
    step = sub // chunks
    g, ti, tj = lax.axis_index("grp"), lax.axis_index("ti"), lax.axis_index("tj")
    x, core = ti // CORES, ti % CORES
    zh, zl = tj // zs, tj % zs
    lin = g * tj_count + tj

    def dev(gg, tt, jj):
        return {"grp": gg, "ti": tt, "tj": jj}

    def owner_dev(k):
        d = lax.rem(lin + k, owners)
        return d, dev(d // tj_count, ti, lax.rem(d, tj_count))

    def row_dev(dx, dy):
        return dev(lax.rem(g + dy, 2), lax.rem(x + dx, xs) * CORES + core, tj)

    def col_dev(dc, dz):
        return dev(g, x * CORES + lax.rem(core + dc, CORES), zh * zs + lax.rem(zl + dz, zs))

    def final_dev(dx, dy):
        return dev(zh, lax.rem(x + dx, xs) * CORES + core, lax.rem(g + dy, 2) * zs + zl)

    def feeder_dev(dx, dy):
        return dev(dy, lax.rem(x + dx, xs) * CORES + core, g * zs + zl)

    barrier = pltpu.get_barrier_semaphore()
    greeted = 0
    targets = [owner_dev(k)[1] for k in range(1, owners)]
    targets += [row_dev(dx, dy) for dx in range(1, xs) for dy in range(2)]
    targets += [col_dev(dc, dz) for dc in range(1, CORES) for dz in range(zs)]
    targets += [final_dev(dx, dy) for dx in range(1, xs) for dy in range(2)]
    targets += [feeder_dev(dx, dy) for dx in range(1, xs) for dy in range(2)]
    for target in targets:
        pl.semaphore_signal(barrier, inc=1, device_id=target, device_id_type=MESH)
        greeted += 1

    v = slots_ref[...]
    member = v >= 0
    second = (v >= cluster).astype(jnp.int32)
    inblk = v - second * cluster - ti * blk
    s = jnp.zeros_like(v)
    for k in range(1, tj_count):
        s = s + (inblk >= k * sub).astype(jnp.int32)
    pos = inblk - s * sub
    s_hi = (s >= zs).astype(jnp.int32)
    owner = s_hi * tj_count + second * zs + s - s_hi * zs
    owner = jnp.where(member, owner, owners)
    piece = 256 if count % 256 == 0 else 128
    before = (
        lax.broadcasted_iota(jnp.int32, (piece, piece), 0)
        < lax.broadcasted_iota(jnp.int32, (piece, piece), 1)
    ).astype(jnp.bfloat16)
    carry = jnp.zeros((owners, 1), jnp.float32)
    owner_iota = lax.broadcasted_iota(jnp.int32, (owners, piece), 0)
    for p in range(count // piece):
        part = slice(p * piece, (p + 1) * piece)
        mine = owner_iota == owner[:, part]
        hot = mine.astype(jnp.float32)
        ranks = dot(hot.astype(jnp.bfloat16), before, NN) + carry
        carry = carry + jnp.sum(hot, axis=1, keepdims=True)
        rank = jnp.sum(jnp.where(mine, ranks, 0.0), axis=0, keepdims=True).astype(jnp.int32)
        spot[:, part] = jnp.where(member[:, part], owner[:, part] * cap + rank, owners * cap)
    line = lax.broadcasted_iota(jnp.int32, (16, count), 0)
    ids_src[...] = jnp.where(
        line == 0, pos >> 5, jnp.where(line == 1, pos & 31, (line == 2).astype(jnp.int32))
    ).astype(jnp.float32).astype(jnp.bfloat16)

    pl.semaphore_wait(barrier, greeted)

    def pack(k):
        d = lax.rem(lin + k, owners)
        pick = (
            spot[...] == d * cap + lax.broadcasted_iota(jnp.int32, (cap, count), 0)
        ).astype(jnp.float32).astype(jnp.bfloat16)
        packed = dot(pick, corpus_ref[0], NN).astype(jnp.bfloat16)
        ids = dot(ids_src[...], pick, NT).astype(jnp.bfloat16)
        return packed, ids

    def row_copy(k):
        return pltpu.make_async_remote_copy(
            send.at[k], got.at[k], s_send.at[k], s_recv.at[k],
            device_id=owner_dev(k)[1], device_id_type=MESH)

    def id_copy(k):
        return pltpu.make_async_remote_copy(
            send_ids.at[k], got_ids.at[k], i_send.at[k], i_recv.at[k],
            device_id=owner_dev(k)[1], device_id_type=MESH)

    def send_step(k, _):
        packed, ids = pack(k)
        send[k] = packed
        send_ids[k, :, :cap] = ids

        @pl.when(k > 1)
        def _():
            id_copy(k - 1).start()
            row_copy(k - 1).start()
        return 0

    lax.fori_loop(1, owners, send_step, 0)
    packed, ids = pack(0)
    got[0] = packed
    got_ids[0, :, :cap] = ids
    id_copy(owners - 1).start()
    row_copy(owners - 1).start()

    def place(k):
        line_ids = got_ids[k, :, :cap].astype(jnp.float32)
        where = (line_ids[0:1] * 32.0 + line_ids[1:2]).astype(jnp.int32)
        where = jnp.where(line_ids[2:3] > 0.5, where, sub)
        pick = (
            where == lax.broadcasted_iota(jnp.int32, (sub, cap), 0)
        ).astype(jnp.float32).astype(jnp.bfloat16)
        return dot(pick, got[k], NN)

    summed[...] = place(0)

    def place_step(k, _):
        id_copy(k).wait_recv()
        row_copy(k).wait_recv()
        summed[...] += place(k)
        return 0

    lax.fori_loop(1, owners, place_step, 0)

    row_peers = [(dx, dy) for dx in range(xs) for dy in range(2)]
    col_peers = [(dc, dz) for dc in range(CORES) for dz in range(zs)]
    row_slot = {peer: i for i, peer in enumerate(row_peers)}
    col_slot = {peer: i for i, peer in enumerate(col_peers)}

    def block_copy(peer, i, is_row):
        part = pl.ds(i * step, step)
        if is_row:
            slot = row_slot[((-peer[0]) % xs, (-peer[1]) % 2)]
            return pltpu.make_async_remote_copy(
                rows.at[0, part], rows.at[slot, part],
                r_send.at[slot, i], r_recv.at[slot, i],
                device_id=row_dev(*peer), device_id_type=MESH)
        slot = col_slot[((-peer[0]) % CORES, (-peer[1]) % zs)]
        return pltpu.make_async_remote_copy(
            cols.at[0, part], cols.at[slot, part],
            c_send.at[slot, i], c_recv.at[slot, i],
            device_id=col_dev(*peer), device_id_type=MESH)

    copies = []

    def launch(i):
        for peer in col_peers[1:]:
            copies.append(block_copy(peer, i, False))
            copies[-1].start()
        for peer in row_peers[1:]:
            copies.append(block_copy(peer, i, True))
            copies[-1].start()

    for i in range(chunks):
        part = slice(i * step, (i + 1) * step)
        wide = summed[part]
        squares = jnp.sum(wide * wide, axis=1, keepdims=True)
        unit = (wide * lax.rsqrt(squares + EPSILON)).astype(jnp.bfloat16)
        rows[0, part] = unit
        cols[0, part] = unit
        if i:
            launch(i - 1)

    best[...] = jnp.full(best.shape, -2.0, jnp.float32)
    launch(chunks - 1)

    def tile(row, i, col, own=False):
        part = pl.ds(pl.multiple_of(i * step, step), step)
        scores = dot(cols[col], rows[row, part, :], NT)
        if own:
            same = (
                lax.broadcasted_iota(jnp.int32, (sub, step), 0)
                == i * step + lax.broadcasted_iota(jnp.int32, (sub, step), 1)
            )
            scores = jnp.where(same, -2.0, scores)
        top = jnp.max(scores.reshape(sub // 8, 8, step), axis=0)
        best[row, i] = jnp.maximum(best[row, i], top)
        return 0

    lax.fori_loop(0, chunks, lambda i, _: tile(0, i, 0, True), 0)
    for col in range(1, len(col_peers)):
        for i in range(chunks):
            block_copy(((-col_peers[col][0]) % CORES, (-col_peers[col][1]) % zs), i, False).wait_recv()
        lax.fori_loop(0, chunks, lambda i, _, col=col: tile(0, i, col), 0)

    def part_copy(row):
        return pltpu.make_async_remote_copy(
            best.at[row], parts.at[x * 2 + g], p_send.at[row], p_recv.at[x * 2 + g],
            device_id=final_dev(*row_peers[row]), device_id_type=MESH)

    stays = zh == g

    @pl.when(stays)
    def _():
        parts[x * 2 + g] = best[0]

    @pl.when(jnp.logical_not(stays))
    def _():
        part_copy(0).start()

    for row in range(1, len(row_peers)):
        peer = row_peers[row]
        for i in range(chunks):
            block_copy(((-peer[0]) % xs, (-peer[1]) % 2), i, True).wait_recv()
            lax.fori_loop(0, len(col_peers), lambda col, _, row=row, i=i: tile(row, i, col), 0)
        part_copy(row).start()

    for feeder in range(len(row_peers)):
        arrived = pltpu.make_async_remote_copy(
            best.at[0], parts.at[feeder], p_send.at[0], p_recv.at[feeder],
            device_id=final_dev(0, 0), device_id_type=MESH)
        if feeder < len(row_peers):
            here = jnp.logical_and(stays, x * 2 + g == feeder)

            @pl.when(jnp.logical_not(here))
            def _(arrived=arrived):
                arrived.wait_recv()
    for i in range(chunks):
        top = jnp.max(parts[:, i], axis=0)
        out_ref[:, i * step : (i + 1) * step] = jnp.max(top, axis=0, keepdims=True)

    @pl.when(jnp.logical_not(stays))
    def _():
        part_copy(0).wait_send()

    for row in range(1, len(row_peers)):
        part_copy(row).wait_send()
    for copy in copies:
        copy.wait_send()

    def drain(k, _):
        id_copy(k).wait_send()
        row_copy(k).wait_send()
        return 0

    lax.fori_loop(1, owners, drain, 0)


def per_device(corpus, slot_of_row):
    ti_count, tj_count = lax.axis_size("ti"), lax.axis_size("tj")
    _, count, features = corpus.shape
    sub = count // 2
    cap = sub // tj_count
    owners = 2 * tj_count
    chunks = 3
    step = sub // chunks
    row_blocks, col_blocks = ti_count // CORES * 2, tj_count // 2 * CORES
    wide_cap = -(-cap // 128) * 128
    dma = pltpu.SemaphoreType.DMA
    vmem = pl.BlockSpec(memory_space=pltpu.VMEM)
    return pl.pallas_call(
        functools.partial(kernel, (ti_count, tj_count, count, features, sub, cap, chunks)),
        out_shape=jax.ShapeDtypeStruct((1, sub), jnp.float32),
        in_specs=[vmem, vmem],
        out_specs=vmem,
        scratch_shapes=[
            pltpu.VMEM((1, count), jnp.int32),
            pltpu.VMEM((16, count), jnp.bfloat16),
            pltpu.VMEM((owners, cap, features), jnp.bfloat16),
            pltpu.VMEM((owners, 16, wide_cap), jnp.bfloat16),
            pltpu.VMEM((owners, cap, features), jnp.bfloat16),
            pltpu.VMEM((owners, 16, wide_cap), jnp.bfloat16),
            pltpu.VMEM((sub, features), jnp.float32),
            pltpu.VMEM((row_blocks, sub, features), jnp.bfloat16),
            pltpu.VMEM((col_blocks, sub, features), jnp.bfloat16),
            pltpu.VMEM((row_blocks, chunks, 8, step), jnp.float32),
            pltpu.VMEM((row_blocks, chunks, 8, step), jnp.float32),
            dma((owners,)), dma((owners,)), dma((owners,)), dma((owners,)),
            dma((row_blocks, chunks)), dma((row_blocks, chunks)),
            dma((col_blocks, chunks)), dma((col_blocks, chunks)),
            dma((row_blocks,)), dma((row_blocks,)),
        ],
        compiler_params=pltpu.CompilerParams(
            collective_id=0, has_side_effects=True, vmem_limit_bytes=60 * 1024 * 1024),
    )(slot_of_row, corpus)


def solution(mesh):
    in_specs = (P("grp", ("ti", "tj"), None), P("grp", ("ti", "tj")))
    out_specs = P("grp", ("ti", "tj"))
    return jax.shard_map(
        per_device, mesh=mesh, in_specs=in_specs, out_specs=out_specs, check_vma=False
    )
```

time: 336 us -> 179 us (0.53)
  waiting for transfers between devices: 230 us -> 0 us
  Pallas kernels: 0 us -> 178 us
  local copies, waits for them, and re-layouts: 27 us -> 1.26 us
  matrix products: 23.7 us -> 0 us
  blocking collectives: 18.7 us -> 0 us
  starting transfers between devices: 13.6 us -> 0 us
  between operations: 13.5 us -> 0.01 us
  other arithmetic: 9.96 us -> 0 us
    pallas_call x0 -> x1, Pallas kernels: none -> 178 us  [per_device(): pl.pallas_call(functools.partial(kernel, (ti_count, tj_count, count, feat...]
    all_gather x2 -> x0, waiting for transfers between devices: 158 us -> none  [the longest x1 112 us: per_device(): block_rows = lax.all_gather(unit_rows, 'tj', axis=0, tiled=True)]
    all_to_all x2 -> x0, waiting for transfers between devices: 70.9 us -> none  [the longest x1 70.9 us: per_device(): lax.all_to_all(send_rows.reshape(owners, capacity, features), ('grp', 'tj...]
    scatter x3 -> x0, local copies, waits for them, and re-layouts: 25.3 us -> none  [the longest x1 9.66 us: per_device(): send_rows = jnp.zeros((owners * capacity, features), rows_in.dtype).at[sl...]
    dot_general x1 -> x0, matrix products: 23.7 us -> none  [per_device(): lax.dot_general(block_rows, portion, (((1,), (1,)), ((), ())), preferred_...]
    pmax x1 -> x0, blocking collectives: 18.7 us -> none  [per_device(): combined = lax.pmax(tile_best, 'tj')]
    all_to_all x2 -> x0, starting transfers between devices: 13.3 us -> none  [the longest x1 7.31 us: per_device(): lax.all_to_all(send_ids.reshape(owners, capacity), ('grp', 'tj'), split_a...]
  transfers between devices with their start and end apart: 4 -> 0, of which waited for: 3 -> 0; matrix products, arithmetic and copies ran while one was open for 3% -> 0% of each run, Pallas kernels for 0% -> 0%
where the time goes in v1:
time: 179 us
  Pallas kernels  178 us (99%)
    pallas_call x1, Pallas kernels, per_device(): pl.pallas_call(functools.partial(kernel, (ti_count, tj_count, count, feat...  178 us

profile of v1, /device:TPU:0, one launch (start us, length us, event | category | flops | bytes accessed | tf_op | source)
XLA Modules:
  0.0 179.2 jit_solution(11993066687932216129)
XLA Ops:
  0.0 177.9 %shard_map.28 = f32[1,768]{1,0:T(1,128)} custom-call(s32[1,1536]{1,0:T(1,128)} %slots_ref.1, bf16[1,1536,1024]{2,1,0:T(8,128)(2,1)} %corpus_ref.1), custom_call_target="tpu_custom_call" | custom-call | tf_op jit(solution)/shard_map/pallas_call | solution.py:281
  178.0 1.3 copy.4

commit v2 on v1

v2 whole, which is shorter than its diff:
```python
import functools

import jax
import jax.numpy as jnp
from jax import lax
from jax.experimental import pallas as pl
from jax.experimental.pallas import tpu as pltpu
from jax.sharding import PartitionSpec as P

MESH = pl.DeviceIdType.MESH
NT = (((1,), (1,)), ((), ()))
NN = (((1,), (0,)), ((), ()))
CORES = 2
EPSILON = 1e-06


def dot(a, b, dims):
    return lax.dot_general(a, b, dims, preferred_element_type=jnp.float32)


def kernel(geo, slots_ref, corpus_ref, out_ref, spot, ids_src, send, send_ids, got, got_ids,
           picks, summed, raw, units, best, parts, s_send, s_recv, i_send, i_recv,
           b_send, b_recv, p_send, p_recv):
    ti_count, tj_count, count, features, sub, cap, chunks, parts_f = geo
    width = features // parts_f
    owners = 2 * tj_count
    xs = ti_count // CORES
    zs = tj_count // 2
    blk = sub * tj_count
    cluster = blk * ti_count
    step = sub // chunks
    g, ti, tj = lax.axis_index("grp"), lax.axis_index("ti"), lax.axis_index("tj")
    x, core = ti // CORES, ti % CORES
    zh, zl = tj // zs, tj % zs
    lin = g * tj_count + tj

    def dev(gg, tt, jj):
        return {"grp": gg, "ti": tt, "tj": jj}

    def owner_dev(k):
        d = lax.rem(lin + k, owners)
        return d, dev(d // tj_count, ti, lax.rem(d, tj_count))

    def row_dev(dx, dy):
        return dev(lax.rem(g + dy, 2), lax.rem(x + dx, xs) * CORES + core, tj)

    def col_dev(dc, dz):
        return dev(g, x * CORES + lax.rem(core + dc, CORES), zh * zs + lax.rem(zl + dz, zs))

    def final_dev(dx, dy):
        return dev(zh, lax.rem(x + dx, xs) * CORES + core, lax.rem(g + dy, 2) * zs + zl)

    def feeder_dev(dx, dy):
        return dev(dy, lax.rem(x + dx, xs) * CORES + core, g * zs + zl)

    barrier = pltpu.get_barrier_semaphore()
    greeted = 0
    targets = [owner_dev(k)[1] for k in range(1, owners)]
    targets += [row_dev(dx, dy) for dx in range(1, xs) for dy in range(2)]
    targets += [col_dev(dc, dz) for dc in range(1, CORES) for dz in range(zs)]
    targets += [final_dev(dx, dy) for dx in range(1, xs) for dy in range(2)]
    targets += [feeder_dev(dx, dy) for dx in range(1, xs) for dy in range(2)]
    for target in targets:
        pl.semaphore_signal(barrier, inc=1, device_id=target, device_id_type=MESH)
        greeted += 1

    v = slots_ref[...]
    member = v >= 0
    second = (v >= cluster).astype(jnp.int32)
    inblk = v - second * cluster - ti * blk
    s = jnp.zeros_like(v)
    for k in range(1, tj_count):
        s = s + (inblk >= k * sub).astype(jnp.int32)
    pos = inblk - s * sub
    s_hi = (s >= zs).astype(jnp.int32)
    owner = s_hi * tj_count + second * zs + s - s_hi * zs
    owner = jnp.where(member, owner, owners)
    piece = 256 if count % 256 == 0 else 128
    before = (
        lax.broadcasted_iota(jnp.int32, (piece, piece), 0)
        < lax.broadcasted_iota(jnp.int32, (piece, piece), 1)
    ).astype(jnp.bfloat16)
    carry = jnp.zeros((owners, 1), jnp.float32)
    owner_iota = lax.broadcasted_iota(jnp.int32, (owners, piece), 0)
    for p in range(count // piece):
        part = slice(p * piece, (p + 1) * piece)
        mine = owner_iota == owner[:, part]
        hot = mine.astype(jnp.float32)
        ranks = dot(hot.astype(jnp.bfloat16), before, NN) + carry
        carry = carry + jnp.sum(hot, axis=1, keepdims=True)
        rank = jnp.sum(jnp.where(mine, ranks, 0.0), axis=0, keepdims=True).astype(jnp.int32)
        spot[:, part] = jnp.where(member[:, part], owner[:, part] * cap + rank, owners * cap)
    line = lax.broadcasted_iota(jnp.int32, (16, count), 0)
    ids_src[...] = jnp.where(
        line == 0, pos >> 5, jnp.where(line == 1, pos & 31, (line == 2).astype(jnp.int32))
    ).astype(jnp.float32).astype(jnp.bfloat16)

    row_peers = [(dx, dy) for dx in range(xs) for dy in range(2)]
    col_peers = [(dc, dz) for dc in range(CORES) for dz in range(zs)]
    own = len(row_peers) - 1
    row_at = {peer: i - 1 if i else own for i, peer in enumerate(row_peers)}
    col_at = {peer: own + i for i, peer in enumerate(col_peers)}
    lanes = [pl.ds(f * width, width) for f in range(parts_f)]
    half = sub // 2

    def pick_of(k):
        d = lax.rem(lin + k, owners)
        return (
            spot[...] == d * cap + lax.broadcasted_iota(jnp.int32, (cap, count), 0)
        ).astype(jnp.float32).astype(jnp.bfloat16)

    def row_copy(k, f):
        return pltpu.make_async_remote_copy(
            send.at[k, :, lanes[f]], got.at[k, :, lanes[f]], s_send.at[k, f], s_recv.at[k, f],
            device_id=owner_dev(k)[1], device_id_type=MESH)

    def id_copy(k):
        return pltpu.make_async_remote_copy(
            send_ids.at[k], got_ids.at[k], i_send.at[k], i_recv.at[k],
            device_id=owner_dev(k)[1], device_id_type=MESH)

    def start_pair(k, f):
        if f == 0:
            id_copy(k).start()
        row_copy(k, f).start()

    def pack(f):
        def one(k, _):
            pick = pick_of(k)
            send[k, :, lanes[f]] = dot(pick, corpus_ref[0, :, lanes[f]], NN).astype(jnp.bfloat16)
            if f == 0:
                send_ids[k, :, :cap] = dot(ids_src[...], pick, NT).astype(jnp.bfloat16)

            @pl.when(k > 1)
            def _():
                start_pair(k - 1, f)
            return 0

        lax.fori_loop(1, owners, one, 0)
        pick = pick_of(0)
        got[0, :, lanes[f]] = dot(pick, corpus_ref[0, :, lanes[f]], NN).astype(jnp.bfloat16)
        if f == 0:
            got_ids[0, :, :cap] = dot(ids_src[...], pick, NT).astype(jnp.bfloat16)
        start_pair(owners - 1, f)

    def place(f):
        def one(k, first):
            if f == 0:
                line_ids = got_ids[k, :, :cap].astype(jnp.float32)
                where = (line_ids[0:1] * 32.0 + line_ids[1:2]).astype(jnp.int32)
                where = jnp.where(line_ids[2:3] > 0.5, where, sub)
                picks[k] = (
                    where == lax.broadcasted_iota(jnp.int32, (sub, cap), 0)
                ).astype(jnp.float32).astype(jnp.bfloat16)
            term = dot(picks[k], got[k, :, lanes[f]], NN)
            summed[...] = term if first else summed[...] + term

        def arrived(k, _):
            if f == 0:
                id_copy(k).wait_recv()
            row_copy(k, f).wait_recv()
            one(k, False)
            return 0

        one(0, True)
        lax.fori_loop(1, owners, arrived, 0)

    started, waited = [], set()

    def block_copy(source, target, f, h, device):
        area = (pl.ds(h * half, half), lanes[f])
        return pltpu.make_async_remote_copy(
            raw.at[(source,) + area], raw.at[(target,) + area],
            b_send.at[target, f, h], b_recv.at[target, f, h],
            device_id=device, device_id_type=MESH)

    def ship(source, target, f, h, device):
        copy = block_copy(source, target, f, h, device)
        copy.start()
        started.append(copy)

    def need(block, f, h):
        if (block, f, h) not in waited:
            waited.add((block, f, h))
            block_copy(own, block, f, h, row_dev(0, 1)).wait_recv()

    def launch(f):
        for n in range(2):
            for dx, dy in row_peers[1:]:
                if xs == 2 and dx and dy:
                    continue
                ship(own, row_at[(-dx) % xs, (-dy) % 2], f, 1 - n if dy else n, row_dev(dx, dy))
            for dc, dz in col_peers[1:]:
                if zs == 2 and dc and dz:
                    continue
                ship(own, col_at[(-dc) % CORES, (-dz) % zs], f, n, col_dev(dc, dz))

    def relay(f):
        if xs == 2:
            need(row_at[1, 0], f, 0)
            ship(row_at[1, 0], row_at[1, 1], f, 0, row_dev(0, 1))
            need(row_at[0, 1], f, 1)
            ship(row_at[0, 1], row_at[1, 1], f, 1, row_dev(1, 0))
        if zs == 2:
            for h in range(2):
                need(col_at[0, 1], f, h)
                ship(col_at[0, 1], col_at[1, 1], f, h, col_dev(1, 0))

    pl.semaphore_wait(barrier, greeted)
    ahead = 2
    for f in range(min(ahead, parts_f)):
        pack(f)
    for f in range(parts_f):
        place(f)
        raw[own, :, lanes[f]] = summed[...].astype(jnp.bfloat16)
        if f == 0:
            best[...] = jnp.full(best.shape, -2.0, jnp.float32)
        if f:
            relay(f - 1)
        launch(f)
        if f + ahead < parts_f:
            pack(f + ahead)

    def norm(block):
        for f in range(parts_f):
            for h in range(2):
                if block != own:
                    need(block, f, h)

        def one(n, _):
            area = pl.ds(pl.multiple_of(n * 128, 128), 128)
            wide = raw[block, area, :].astype(jnp.float32)
            squares = jnp.sum(wide * wide, axis=1, keepdims=True)
            units[block, area, :] = (wide * lax.rsqrt(squares + EPSILON)).astype(jnp.bfloat16)
            return 0

        lax.fori_loop(0, sub // 128, one, 0)

    def tile(row, i, col, diagonal=False):
        part = pl.ds(pl.multiple_of(i * step, step), step)
        scores = dot(units[own + col], units[row, part, :], NT)
        if diagonal:
            same = (
                lax.broadcasted_iota(jnp.int32, (sub, step), 0)
                == i * step + lax.broadcasted_iota(jnp.int32, (sub, step), 1)
            )
            scores = jnp.where(same, -2.0, scores)
        top = jnp.max(scores.reshape(sub // 8, 8, step), axis=0)
        best[row, i] = jnp.maximum(best[row, i], top)
        return 0

    norm(own)
    lax.fori_loop(0, chunks, lambda i, _: tile(own, i, 0, True), 0)
    relay(parts_f - 1)
    for col in range(1, len(col_peers)):
        norm(own + col)
        lax.fori_loop(0, chunks, lambda i, _, col=col: tile(own, i, col), 0)

    def part_copy(peer):
        return pltpu.make_async_remote_copy(
            best.at[row_at[peer]], parts.at[x * 2 + g],
            p_send.at[row_at[peer]], p_recv.at[x * 2 + g],
            device_id=final_dev(*peer), device_id_type=MESH)

    stays = zh == g

    @pl.when(stays)
    def _():
        parts[x * 2 + g] = best[own]

    @pl.when(jnp.logical_not(stays))
    def _():
        part_copy((0, 0)).start()

    order = [peer for peer in row_peers[1:] if not (peer[0] and peer[1])]
    order += [peer for peer in row_peers[1:] if peer[0] and peer[1]]
    total = chunks * len(col_peers)
    for peer in order:
        row = row_at[peer]
        norm(row)
        lax.fori_loop(
            0, total, lambda n, _, row=row: tile(row, n // len(col_peers), n % len(col_peers)), 0)
        part_copy(peer).start()

    for feeder in range(len(row_peers)):
        arrived = pltpu.make_async_remote_copy(
            best.at[0], parts.at[feeder], p_send.at[0], p_recv.at[feeder],
            device_id=row_dev(0, 1), device_id_type=MESH)
        here = jnp.logical_and(stays, x * 2 + g == feeder)

        @pl.when(jnp.logical_not(here))
        def _(arrived=arrived):
            arrived.wait_recv()
    for i in range(chunks):
        top = jnp.max(parts[:, i], axis=0)
        out_ref[:, i * step : (i + 1) * step] = jnp.max(top, axis=0, keepdims=True)

    @pl.when(jnp.logical_not(stays))
    def _():
        part_copy((0, 0)).wait_send()

    for peer in row_peers[1:]:
        part_copy(peer).wait_send()
    for copy in started:
        copy.wait_send()

    def drain(k, _):
        id_copy(k).wait_send()
        for f in range(parts_f):
            row_copy(k, f).wait_send()
        return 0

    lax.fori_loop(1, owners, drain, 0)


def per_device(corpus, slot_of_row):
    ti_count, tj_count = lax.axis_size("ti"), lax.axis_size("tj")
    _, count, features = corpus.shape
    sub = count // 2
    cap = sub // tj_count
    owners = 2 * tj_count
    chunks, parts_f = 3, 4
    step = sub // chunks
    row_blocks, col_blocks = ti_count // CORES * 2, tj_count // 2 * CORES
    blocks = row_blocks + col_blocks - 1
    wide_cap = -(-cap // 128) * 128
    dma = pltpu.SemaphoreType.DMA
    vmem = pl.BlockSpec(memory_space=pltpu.VMEM)
    return pl.pallas_call(
        functools.partial(kernel, (ti_count, tj_count, count, features, sub, cap, chunks, parts_f)),
        out_shape=jax.ShapeDtypeStruct((1, sub), jnp.float32),
        in_specs=[vmem, vmem],
        out_specs=vmem,
        scratch_shapes=[
            pltpu.VMEM((1, count), jnp.int32),
            pltpu.VMEM((16, count), jnp.bfloat16),
            pltpu.VMEM((owners, cap, features), jnp.bfloat16),
            pltpu.VMEM((owners, 16, wide_cap), jnp.bfloat16),
            pltpu.VMEM((owners, cap, features), jnp.bfloat16),
            pltpu.VMEM((owners, 16, wide_cap), jnp.bfloat16),
            pltpu.VMEM((owners, sub, cap), jnp.bfloat16),
            pltpu.VMEM((sub, features // parts_f), jnp.float32),
            pltpu.VMEM((blocks, sub, features), jnp.bfloat16),
            pltpu.VMEM((blocks, sub, features), jnp.bfloat16),
            pltpu.VMEM((row_blocks, chunks, 8, step), jnp.float32),
            pltpu.VMEM((row_blocks, chunks, 8, step), jnp.float32),
            dma((owners, parts_f)), dma((owners, parts_f)), dma((owners,)), dma((owners,)),
            dma((blocks, parts_f, 2)), dma((blocks, parts_f, 2)),
            dma((row_blocks,)), dma((row_blocks,)),
        ],
        compiler_params=pltpu.CompilerParams(
            collective_id=0, has_side_effects=True, vmem_limit_bytes=60 * 1024 * 1024),
    )(slot_of_row, corpus)


def solution(mesh):
    in_specs = (P("grp", ("ti", "tj"), None), P("grp", ("ti", "tj")))
    out_specs = P("grp", ("ti", "tj"))
    return jax.shard_map(
        per_device, mesh=mesh, in_specs=in_specs, out_specs=out_specs, check_vma=False
    )
```

time: 179 us -> 140 us (0.78)
  Pallas kernels: 178 us -> 139 us
    pallas_call x1, Pallas kernels: 178 us -> 139 us  [per_device(): pl.pallas_call(functools.partial(kernel, (ti_count, tj_count, count, feat...]
where the time goes in v2:
time: 140 us
  Pallas kernels  139 us (99%)
    pallas_call x1, Pallas kernels, per_device(): pl.pallas_call(functools.partial(kernel, (ti_count, tj_count, count, feat...  139 us

profile of v2, /device:TPU:0, one launch (start us, length us, event | category | flops | bytes accessed | tf_op | source)
XLA Modules:
  0.0 140.0 jit_solution(8180058789885259140)
XLA Ops:
  0.0 138.7 %shard_map.28 = f32[1,768]{1,0:T(1,128)} custom-call(s32[1,1536]{1,0:T(1,128)} %slots_ref.1, bf16[1,1536,1024]{2,1,0:T(8,128)(2,1)} %corpus_ref.1), custom_call_target="tpu_custom_call" | custom-call | tf_op jit(solution)/shard_map/pallas_call | solution.py:329
  138.7 1.3 copy.4

commit v3 on v2

--- a/solution.py
+++ b/solution.py
@@ -319,7 +319,7 @@
     sub = count // 2
     cap = sub // tj_count
     owners = 2 * tj_count
-    chunks, parts_f = 3, 4
+    chunks, parts_f = 1, 4
     step = sub // chunks
     row_blocks, col_blocks = ti_count // CORES * 2, tj_count // 2 * CORES
     blocks = row_blocks + col_blocks - 1

time: 140 us -> 136 us (0.971)
  Pallas kernels: 139 us -> 134 us
    pallas_call x1, Pallas kernels: 139 us -> 134 us  [per_device(): pl.pallas_call(functools.partial(kernel, (ti_count, tj_count, count, feat...]
where the time goes in v3:
time: 136 us; the launch traced here: 135 us
  Pallas kernels  134 us (99%)
    pallas_call x1, Pallas kernels, per_device(): pl.pallas_call(functools.partial(kernel, (ti_count, tj_count, count, feat...  134 us

profile of v3, /device:TPU:0, one launch (start us, length us, event | category | flops | bytes accessed | tf_op | source)
XLA Modules:
  0.0 135.3 jit_solution(3790465182515970494)
XLA Ops:
  0.0 134.1 %shard_map.28 = f32[1,768]{1,0:T(1,128)} custom-call(s32[1,1536]{1,0:T(1,128)} %slots_ref.1, bf16[1,1536,1024]{2,1,0:T(8,128)(2,1)} %corpus_ref.1), custom_call_target="tpu_custom_call" | custom-call | tf_op jit(solution)/shard_map/pallas_call | solution.py:329
  134.1 1.3 copy.4
